TPU v7x, 128 devices: a whole 4x4x4 slice. The times are simulated.
128 devices in a mesh: nodes: 16 (over x, z), cols: 8 (over y, core).
Axes of the slice: x: 4, y: 4, z: 4, core: 2. Of those that a mesh axis runs over, the one named last changes fastest.
Arguments:
- node_feats: bfloat16 [32768, 256], P(('nodes', 'cols')), may hold values from -6 to 6
- tile_row: int32 [16, 2816], P('nodes', 'cols'), may hold values from 0 to 15, as said below
- tile_col: int32 [16, 2816], P('nodes', 'cols'), may hold values from 0 to 31
- tile_bits: int32 [16, 2816, 16, 128], P('nodes', 'cols'), may hold values from 0 to 255, as said below
- w_self: bfloat16 [256, 256], replicated, may hold values from -0.375 to 0.375
- w_neigh: bfloat16 [256, 256], replicated, may hold values from -1.5 to 1.5
- bias: float32 [256], replicated, may hold values from -3 to 3
- cotangent: bfloat16 [32768, 256], P(('nodes', 'cols')), may hold values from -6 to 6
Outputs:
- layer_out: bfloat16 [32768, 256], P(('nodes', 'cols'))
- feat_grad: bfloat16 [32768, 256], P(('nodes', 'cols'))
- self_grad: float32 [256, 256], replicated
- neigh_grad: float32 [256, 256], replicated
- bias_grad: float32 [256], replicated
Inputs may be any that keep to these rules, and one draw needn't show every extreme that they name: `tile_row`: destination row block of a tile within its nodes group; in every nodes group at least one block carries no tile. `tile_col`: source row block of a tile within its cols index; a block may carry several tiles. `tile_bits`: bit j of word (w, a) of a tile is its edge from destination row a to source column 8 w + j; bits above the eighth are zero; some destination rows have no edge in any tile.
All inputs are finite; a program needn't handle non-finite values.
Results may differ from a plain program's by a relative error of at most 0.0075.
Values may be sent and summed in bfloat16 or wider, within the bound.
No kernel may reach another device: no remote copies, remote signals or barrier semaphores. Data moves between devices by JAX's collectives and lax.ppermute only.
A program may use at most 64 MiB of HBM per device.

v0:
```python
import math
import jax
import jax.numpy as jnp
from jax import lax
from jax.sharding import PartitionSpec as P


def unpack_tiles(packed):
    shifts = jnp.arange(8, dtype=jnp.int32)
    edge_flags = jnp.right_shift(packed[:, :, None, :], shifts[None, None, :, None]) & 1
    return edge_flags.reshape(packed.shape[0], 128, 128)


def shards(node_feats, tile_row, tile_col, tile_bits, w_self, w_neigh, bias, cotangent):
    rows_dev = node_feats.shape[0]
    width_in = node_feats.shape[1]
    node_count = lax.axis_size("nodes")
    col_count = lax.axis_size("cols")
    per_dev = rows_dev // 128
    dest_count = col_count * per_dev
    source_count = node_count * per_dev
    tile_count = tile_row.shape[1]
    tile_group = math.gcd(tile_count, 32)
    group_count = tile_count // tile_group
    rows_here = tile_row[0].reshape(group_count, tile_group)
    cols_here = tile_col[0].reshape(group_count, tile_group)
    packed_here = tile_bits[0].reshape(group_count, tile_group, 16, 128)
    source = lax.all_gather(node_feats, "nodes", axis=0, tiled=True)
    source_blocks = source.reshape(source_count, 128, width_in)

    def forward_step(totals, tile_set):
        summed, degree = totals
        rows_blk, cols_blk, packed_blk = tile_set
        edge_flags = unpack_tiles(packed_blk)
        bits_blk = edge_flags.astype(jnp.bfloat16)
        picked = source_blocks[cols_blk]
        products = jnp.einsum("tba,tbf->taf", bits_blk, picked, preferred_element_type=jnp.float32)
        summed = summed.at[rows_blk].add(products)
        degree = degree.at[rows_blk].add(jnp.sum(edge_flags, axis=1).astype(jnp.float32))
        return ((summed, degree), None)

    initial = (
        jnp.zeros((dest_count, 128, width_in), jnp.float32),
        jnp.zeros((dest_count, 128), jnp.float32),
    )
    (partial_sum, degree_part), _ = lax.scan(
        forward_step, initial, (rows_here, cols_here, packed_here)
    )
    summed, degree = (
        lax.psum_scatter(
            partial_sum.reshape(dest_count * 128, width_in), "cols", scatter_dimension=0, tiled=True
        ),
        lax.psum_scatter(
            degree_part.reshape(dest_count * 128), "cols", scatter_dimension=0, tiled=True
        ),
    )
    degree = jnp.maximum(degree, 1.0)
    neigh_mean = (summed / degree[:, None]).astype(jnp.bfloat16)
    preact = (
        jnp.dot(node_feats, w_self, preferred_element_type=jnp.float32)
        + jnp.dot(neigh_mean, w_neigh, preferred_element_type=jnp.float32)
        + bias
    )
    sigmoid_pre = jax.nn.sigmoid(preact)
    layer_out = (preact * sigmoid_pre).astype(jnp.bfloat16)
    pre_grad = (
        cotangent.astype(jnp.float32) * sigmoid_pre * (1.0 + preact * (1.0 - sigmoid_pre))
    ).astype(jnp.bfloat16)
    self_term = jnp.dot(node_feats.T, pre_grad, preferred_element_type=jnp.float32)
    neigh_term = jnp.dot(neigh_mean.T, pre_grad, preferred_element_type=jnp.float32)
    bias_term = jnp.sum(pre_grad.astype(jnp.float32), axis=0)
    self_grad, neigh_grad, bias_grad = lax.psum(
        (self_term, neigh_term, bias_term), ("nodes", "cols")
    )
    mean_grad = (
        jnp.dot(pre_grad, w_neigh.T, preferred_element_type=jnp.float32) / degree[:, None]
    ).astype(jnp.bfloat16)
    dest_grad = lax.all_gather(mean_grad, "cols", axis=0, tiled=True)
    grad_blocks = dest_grad.reshape(dest_count, 128, width_in)

    def backward_step(src_grad, tile_set):
        rows_blk, cols_blk, packed_blk = tile_set
        bits_blk = unpack_tiles(packed_blk).astype(jnp.bfloat16)
        picked = grad_blocks[rows_blk]
        products = jnp.einsum("tba,taf->tbf", bits_blk, picked, preferred_element_type=jnp.float32)
        return (src_grad.at[cols_blk].add(products), None)

    src_total, _ = lax.scan(
        backward_step,
        jnp.zeros((source_count, 128, width_in), jnp.float32),
        (rows_here, cols_here, packed_here),
    )
    src_total = src_total.reshape(source_count * 128, width_in)
    src_grad = lax.psum_scatter(src_total, "nodes", scatter_dimension=0, tiled=True)
    feat_grad = (jnp.dot(pre_grad, w_self.T, preferred_element_type=jnp.float32) + src_grad).astype(
        jnp.bfloat16
    )
    return (layer_out, feat_grad, self_grad, neigh_grad, bias_grad)


def solution(mesh):
    return jax.shard_map(
        shards,
        mesh=mesh,
        in_specs=(
            P(("nodes", "cols"), None),
            P("nodes", "cols"),
            P("nodes", "cols"),
            P("nodes", "cols", None, None),
            P(),
            P(),
            P(),
            P(("nodes", "cols"), None),
        ),
        out_specs=(P(("nodes", "cols"), None), P(("nodes", "cols"), None), P(), P(), P()),
        check_vma=False,
    )
```

profile of v0, /device:TPU:0, one launch (start us, length us, event | category | flops | bytes accessed | tf_op | source)
XLA Modules:
  0.0 557.2 jit_solution(13627646105467495376)
XLA Ops:
  9.5 48.4 %all-gather.3.cloned.1.call-done = bf16[4096,256]{1,0:T(8,128)(2,1)} async-done(((bf16[256,256]{1,0:T(8,128)(2,1)}), bf16[4096,256]{1,0:T(8,128)(2,1)}) %all-gather.3.cloned.1.call-update) | async-done | bytes 2097168 | tf_op jit(solution)/shard_map/all_gather | solution.py:28
  58.1 182.1 %while.22 = (s32[]{:T(128)}, f32[16,128,256]{2,1,0:T(8,128)S(1)}, f32[16,128]{1,0:T(8,128)S(1)}, s32[11,32]{1,0:T(8,128)S(1)}, s32[11,32,16,128]{3,2,1,0:T(8,128...) while((s32[]{:T(128)}, f32[16,128,256]{2,1,0:T(8,128)S(1)}, ...), condition=%wide.region_4.5_spmd, body=%wide.region_0.4_spmd.sunk | while | flops 272635072 | bytes 24165348 | solution.py:46
  67.2 6.5 %scatter_fusion = f32[16,128,256]{2,1,0:T(8,128)S(1)} fusion(f32[16,128,256]{2,1,0:T(8,128)S(1)} %get-tuple-element.232, s32[32]{0:T(128)S(1)} %get-tuple-element.213, f32[32,128,256]{2,1,0:T(8,128)} %fusion.56), kind=kCustom, calls=%fused_computation.2.clone.1 | custom fusion | flops 1048576 | bytes 12583040 | tf_op jit(solution)/shard_map/while/body/eval_jaxpr/scatter-add | solution.py:38
  83.8 6.5 %scatter_fusion = f32[16,128,256]{2,1,0:T(8,128)S(1)} fusion(f32[16,128,256]{2,1,0:T(8,128)S(1)} %get-tuple-element.232, s32[32]{0:T(128)S(1)} %get-tuple-element.213, f32[32,128,256]{2,1,0:T(8,128)} %fusion.56), kind=kCustom, calls=%fused_computation.2.clone.1 | custom fusion | flops 1048576 | bytes 12583040 | tf_op jit(solution)/shard_map/while/body/eval_jaxpr/scatter-add | solution.py:38
  100.4 6.5 %scatter_fusion = f32[16,128,256]{2,1,0:T(8,128)S(1)} fusion(f32[16,128,256]{2,1,0:T(8,128)S(1)} %get-tuple-element.232, s32[32]{0:T(128)S(1)} %get-tuple-element.213, f32[32,128,256]{2,1,0:T(8,128)} %fusion.56), kind=kCustom, calls=%fused_computation.2.clone.1 | custom fusion | flops 1048576 | bytes 12583040 | tf_op jit(solution)/shard_map/while/body/eval_jaxpr/scatter-add | solution.py:38
  112.5 4.4 fusion.56
  116.9 6.5 %scatter_fusion = f32[16,128,256]{2,1,0:T(8,128)S(1)} fusion(f32[16,128,256]{2,1,0:T(8,128)S(1)} %get-tuple-element.232, s32[32]{0:T(128)S(1)} %get-tuple-element.213, f32[32,128,256]{2,1,0:T(8,128)} %fusion.56), kind=kCustom, calls=%fused_computation.2.clone.1 | custom fusion | flops 1048576 | bytes 12583040 | tf_op jit(solution)/shard_map/while/body/eval_jaxpr/scatter-add | solution.py:38
  133.5 6.5 %scatter_fusion = f32[16,128,256]{2,1,0:T(8,128)S(1)} fusion(f32[16,128,256]{2,1,0:T(8,128)S(1)} %get-tuple-element.232, s32[32]{0:T(128)S(1)} %get-tuple-element.213, f32[32,128,256]{2,1,0:T(8,128)} %fusion.56), kind=kCustom, calls=%fused_computation.2.clone.1 | custom fusion | flops 1048576 | bytes 12583040 | tf_op jit(solution)/shard_map/while/body/eval_jaxpr/scatter-add | solution.py:38
  150.0 6.5 %scatter_fusion = f32[16,128,256]{2,1,0:T(8,128)S(1)} fusion(f32[16,128,256]{2,1,0:T(8,128)S(1)} %get-tuple-element.232, s32[32]{0:T(128)S(1)} %get-tuple-element.213, f32[32,128,256]{2,1,0:T(8,128)} %fusion.56), kind=kCustom, calls=%fused_computation.2.clone.1 | custom fusion | flops 1048576 | bytes 12583040 | tf_op jit(solution)/shard_map/while/body/eval_jaxpr/scatter-add | solution.py:38
  166.6 6.5 %scatter_fusion = f32[16,128,256]{2,1,0:T(8,128)S(1)} fusion(f32[16,128,256]{2,1,0:T(8,128)S(1)} %get-tuple-element.232, s32[32]{0:T(128)S(1)} %get-tuple-element.213, f32[32,128,256]{2,1,0:T(8,128)} %fusion.56), kind=kCustom, calls=%fused_computation.2.clone.1 | custom fusion | flops 1048576 | bytes 12583040 | tf_op jit(solution)/shard_map/while/body/eval_jaxpr/scatter-add | solution.py:38
  178.7 4.4 fusion.56
  183.1 6.5 %scatter_fusion = f32[16,128,256]{2,1,0:T(8,128)S(1)} fusion(f32[16,128,256]{2,1,0:T(8,128)S(1)} %get-tuple-element.232, s32[32]{0:T(128)S(1)} %get-tuple-element.213, f32[32,128,256]{2,1,0:T(8,128)} %fusion.56), kind=kCustom, calls=%fused_computation.2.clone.1 | custom fusion | flops 1048576 | bytes 12583040 | tf_op jit(solution)/shard_map/while/body/eval_jaxpr/scatter-add | solution.py:38
  199.7 6.5 %scatter_fusion = f32[16,128,256]{2,1,0:T(8,128)S(1)} fusion(f32[16,128,256]{2,1,0:T(8,128)S(1)} %get-tuple-element.232, s32[32]{0:T(128)S(1)} %get-tuple-element.213, f32[32,128,256]{2,1,0:T(8,128)} %fusion.56), kind=kCustom, calls=%fused_computation.2.clone.1 | custom fusion | flops 1048576 | bytes 12583040 | tf_op jit(solution)/shard_map/while/body/eval_jaxpr/scatter-add | solution.py:38
  216.2 6.5 %scatter_fusion = f32[16,128,256]{2,1,0:T(8,128)S(1)} fusion(f32[16,128,256]{2,1,0:T(8,128)S(1)} %get-tuple-element.232, s32[32]{0:T(128)S(1)} %get-tuple-element.213, f32[32,128,256]{2,1,0:T(8,128)} %fusion.56), kind=kCustom, calls=%fused_computation.2.clone.1 | custom fusion | flops 1048576 | bytes 12583040 | tf_op jit(solution)/shard_map/while/body/eval_jaxpr/scatter-add | solution.py:38
  232.8 6.5 %scatter_fusion = f32[16,128,256]{2,1,0:T(8,128)S(1)} fusion(f32[16,128,256]{2,1,0:T(8,128)S(1)} %get-tuple-element.232, s32[32]{0:T(128)S(1)} %get-tuple-element.213, f32[32,128,256]{2,1,0:T(8,128)} %fusion.56), kind=kCustom, calls=%fused_computation.2.clone.1 | custom fusion | flops 1048576 | bytes 12583040 | tf_op jit(solution)/shard_map/while/body/eval_jaxpr/scatter-add | solution.py:38
  243.1 13.7 %all-reduce = f32[2048]{0:T(1024)S(1)} all-reduce(f32[2048]{0:T(1024)S(1)} %bitcast.96), channel_id=3, replica_groups=mesh['nodes'=16,'cols'=8] {'cols'}, use_global_device_ids=true, to_apply=%region_6.7.clone | all-reduce | flops 2048 | bytes 16384
  256.9 17.8 %reduce-scatter.3.cloned.1.call-done = f32[256,256]{1,0:T(8,128)} async-done(((f32[2048,256]{1,0:T(8,128)}), f32[256,256]{1,0:T(8,128)}) %reduce-scatter.3.cloned.1.call-update) | async-done | bytes 262160 | tf_op jit(solution)/shard_map/reduce_scatter | solution.py:50
  280.3 20.2 %all-gather.5.cloned.1.call-done = bf16[2048,256]{1,0:T(8,128)(2,1)} async-done(((bf16[256,256]{1,0:T(8,128)(2,1)}), bf16[2048,256]{1,0:T(8,128)(2,1)}) %all-gather.5.cloned.1.call-update) | async-done | bytes 1048592 | tf_op jit(solution)/shard_map/all_gather | solution.py:78
  302.9 166.3 %while.23 = (s32[]{:T(128)}, f32[32,128,256]{2,1,0:T(8,128)}, s32[11,32]{1,0:T(8,128)}, s32[11,32,16,128]{3,2,1,0:T(8,128)}, s32[11,32]{1,0:T(8,128)}, /*index=5*/bf16[16,128,256]{2,1,0:T(8,128)(2,1)S(1)}, s32[]{:T(128)}) while((s32[]{:T(128)}, f32[32,128,256]{2,1,0:T(8,128)}, s32[11,32]{1,0:T(8,128)}, s32[11,32,16,128]{3,2,1,0:T(8,128)}, ...), condition=%wide.region_9.10_spmd, body=%wide.region_7.9_spmd.sunk | while | flops 271058112 | bytes 23862236 | solution.py:88
  308.1 9.9 %scatter_fusion.1 = f32[32,128,256]{2,1,0:T(8,128)} fusion(f32[32,128,256]{2,1,0:T(8,128)} %get-tuple-element.255, s32[32]{0:T(128)S(1)} %get-tuple-element.221, f32[32,128,256]{2,1,0:T(8,128)} %fusion.60), kind=kCustom, calls=%fused_computation.4.clone.1 | custom fusion | flops 1048576 | bytes 12583040 | tf_op jit(solution)/shard_map/while/body/eval_jaxpr/scatter-add | solution.py:86
  323.2 9.9 %scatter_fusion.1 = f32[32,128,256]{2,1,0:T(8,128)} fusion(f32[32,128,256]{2,1,0:T(8,128)} %get-tuple-element.255, s32[32]{0:T(128)S(1)} %get-tuple-element.221, f32[32,128,256]{2,1,0:T(8,128)} %fusion.60), kind=kCustom, calls=%fused_computation.4.clone.1 | custom fusion | flops 1048576 | bytes 12583040 | tf_op jit(solution)/shard_map/while/body/eval_jaxpr/scatter-add | solution.py:86
  338.3 9.9 %scatter_fusion.1 = f32[32,128,256]{2,1,0:T(8,128)} fusion(f32[32,128,256]{2,1,0:T(8,128)} %get-tuple-element.255, s32[32]{0:T(128)S(1)} %get-tuple-element.221, f32[32,128,256]{2,1,0:T(8,128)} %fusion.60), kind=kCustom, calls=%fused_computation.4.clone.1 | custom fusion | flops 1048576 | bytes 12583040 | tf_op jit(solution)/shard_map/while/body/eval_jaxpr/scatter-add | solution.py:86
  353.3 9.9 %scatter_fusion.1 = f32[32,128,256]{2,1,0:T(8,128)} fusion(f32[32,128,256]{2,1,0:T(8,128)} %get-tuple-element.255, s32[32]{0:T(128)S(1)} %get-tuple-element.221, f32[32,128,256]{2,1,0:T(8,128)} %fusion.60), kind=kCustom, calls=%fused_computation.4.clone.1 | custom fusion | flops 1048576 | bytes 12583040 | tf_op jit(solution)/shard_map/while/body/eval_jaxpr/scatter-add | solution.py:86
  368.4 9.9 %scatter_fusion.1 = f32[32,128,256]{2,1,0:T(8,128)} fusion(f32[32,128,256]{2,1,0:T(8,128)} %get-tuple-element.255, s32[32]{0:T(128)S(1)} %get-tuple-element.221, f32[32,128,256]{2,1,0:T(8,128)} %fusion.60), kind=kCustom, calls=%fused_computation.4.clone.1 | custom fusion | flops 1048576 | bytes 12583040 | tf_op jit(solution)/shard_map/while/body/eval_jaxpr/scatter-add | solution.py:86
  383.5 10.0 %scatter_fusion.1 = f32[32,128,256]{2,1,0:T(8,128)} fusion(f32[32,128,256]{2,1,0:T(8,128)} %get-tuple-element.255, s32[32]{0:T(128)S(1)} %get-tuple-element.221, f32[32,128,256]{2,1,0:T(8,128)} %fusion.60), kind=kCustom, calls=%fused_computation.4.clone.1 | custom fusion | flops 1048576 | bytes 12583040 | tf_op jit(solution)/shard_map/while/body/eval_jaxpr/scatter-add | solution.py:86
  398.7 10.2 %scatter_fusion.1 = f32[32,128,256]{2,1,0:T(8,128)} fusion(f32[32,128,256]{2,1,0:T(8,128)} %get-tuple-element.255, s32[32]{0:T(128)S(1)} %get-tuple-element.221, f32[32,128,256]{2,1,0:T(8,128)} %fusion.60), kind=kCustom, calls=%fused_computation.4.clone.1 | custom fusion | flops 1048576 | bytes 12583040 | tf_op jit(solution)/shard_map/while/body/eval_jaxpr/scatter-add | solution.py:86
  414.1 9.9 %scatter_fusion.1 = f32[32,128,256]{2,1,0:T(8,128)} fusion(f32[32,128,256]{2,1,0:T(8,128)} %get-tuple-element.255, s32[32]{0:T(128)S(1)} %get-tuple-element.221, f32[32,128,256]{2,1,0:T(8,128)} %fusion.60), kind=kCustom, calls=%fused_computation.4.clone.1 | custom fusion | flops 1048576 | bytes 12583040 | tf_op jit(solution)/shard_map/while/body/eval_jaxpr/scatter-add | solution.py:86
  429.1 10.0 %scatter_fusion.1 = f32[32,128,256]{2,1,0:T(8,128)} fusion(f32[32,128,256]{2,1,0:T(8,128)} %get-tuple-element.255, s32[32]{0:T(128)S(1)} %get-tuple-element.221, f32[32,128,256]{2,1,0:T(8,128)} %fusion.60), kind=kCustom, calls=%fused_computation.4.clone.1 | custom fusion | flops 1048576 | bytes 12583040 | tf_op jit(solution)/shard_map/while/body/eval_jaxpr/scatter-add | solution.py:86
  444.3 9.9 %scatter_fusion.1 = f32[32,128,256]{2,1,0:T(8,128)} fusion(f32[32,128,256]{2,1,0:T(8,128)} %get-tuple-element.255, s32[32]{0:T(128)S(1)} %get-tuple-element.221, f32[32,128,256]{2,1,0:T(8,128)} %fusion.60), kind=kCustom, calls=%fused_computation.4.clone.1 | custom fusion | flops 1048576 | bytes 12583040 | tf_op jit(solution)/shard_map/while/body/eval_jaxpr/scatter-add | solution.py:86
  459.4 9.8 %scatter_fusion.1 = f32[32,128,256]{2,1,0:T(8,128)} fusion(f32[32,128,256]{2,1,0:T(8,128)} %get-tuple-element.255, s32[32]{0:T(128)S(1)} %get-tuple-element.221, f32[32,128,256]{2,1,0:T(8,128)} %fusion.60), kind=kCustom, calls=%fused_computation.4.clone.1 | custom fusion | flops 1048576 | bytes 12583040 | tf_op jit(solution)/shard_map/while/body/eval_jaxpr/scatter-add | solution.py:86
  469.8 66.2 %psum.23 = f32[256]{0:T(256)} all-reduce(f32[256]{0:T(256)S(1)} %copy-done.7), channel_id=1, replica_groups=mesh['nodes'=16,'cols'=8] {'nodes','cols'}, use_global_device_ids=true, to_apply=%region_14.15 | all-reduce | flops 256 | bytes 2048 | tf_op jit(solution)/shard_map/psum | solution.py:72
  537.9 9.3 %reduce-scatter.5.cloned.1.call-done = f32[256,256]{1,0:T(8,128)} async-done(((f32[4096,256]{1,0:T(8,128)}), f32[256,256]{1,0:T(8,128)}) %reduce-scatter.5.cloned.1.call-update) | async-done | bytes 262160 | tf_op jit(solution)/shard_map/reduce_scatter | solution.py:94
  (226 shorter events, 177.1 us)
Async XLA Ops:
  7.2 267.5 %copy-start = (bf16[256,256]{1,0:T(8,128)(2,1)S(1)}, bf16[256,256]{1,0:T(8,128)(2,1)}, u32[]{:S(2)}) copy-start(bf16[256,256]{1,0:T(8,128)(2,1)} %param.17) | copy-start | bytes 393220
  7.2 50.7 %all-gather.3.cloned.1.call-start = ((), (), s32[]{:S(2)}) async-start(), calls=%async_computation.2 | async-start | bytes 2228224 | tf_op jit(solution)/shard_map/all_gather | solution.py:28
  7.9 266.8 %reduce-scatter.3.cloned.1.call-start = ((), (), s32[]{:S(2)}) async-start(), calls=%async_computation.3 | async-start | bytes 2359296 | tf_op jit(solution)/shard_map/reduce_scatter | solution.py:50
  240.2 1.4 copy-start.1
  240.2 2.0 copy-start.5
  240.2 2.0 copy-start.6
  240.3 1.4 copy-start.11
  240.3 2.6 copy-start.3
  240.3 2.6 copy-start.4
  240.3 34.4 %copy-start.9 = (bf16[256,256]{1,0:T(8,128)(2,1)S(1)}, bf16[256,256]{1,0:T(8,128)(2,1)}, u32[]{:S(2)}) copy-start(bf16[256,256]{1,0:T(8,128)(2,1)} %param.19) | copy-start | bytes 393220
  240.3 34.4 %copy-start.10 = (f32[256]{0:T(256)S(1)}, f32[256]{0:T(256)}, u32[]{:S(2)}) copy-start(f32[256]{0:T(256)} %param.18) | copy-start | bytes 3076
  241.6 58.9 %all-gather.5.cloned.1.call-start = ((), (), s32[]{:S(2)}) async-start(), calls=%async_computation.4 | async-start | bytes 1179648 | tf_op jit(solution)/shard_map/all_gather | solution.py:78
  274.7 4.5 copy-start.8
  278.2 257.9 %all-reduce.4.cloned.1.call-start = ((), (), s32[]{:S(2)}) async-start(), calls=%async_computation.6 | async-start | bytes 1048576 | tf_op jit(solution)/shard_map/psum | solution.py:72
  280.2 267.0 %reduce-scatter.5.cloned.1.call-start = ((), (), s32[]{:S(2)}) async-start(), calls=%async_computation.5 | async-start | bytes 4456448 | tf_op jit(solution)/shard_map/reduce_scatter | solution.py:94
  300.5 2.4 copy-start.2
  469.2 0.7 copy-start.7
Sparse Core Ops, SparseCore 0:
  10.2 47.7 all-gather.2
  241.7 32.9 reduce-scatter.2
  278.3 22.1 all-gather.4
  305.8 144.6 all-reduce.3
  469.3 77.8 reduce-scatter.4
where the time goes:
time: 560 us; the launch traced here: 557 us
  other arithmetic  200 us (36%)
  waiting for transfers between devices  96.4 us (17%)
  matrix products  85.6 us (15%)
  blocking collectives  80 us (14%)
  local copies, waits for them, and re-layouts  79.4 us (14%)
  between operations  14.6 us (3%)
    scatter-add x11, other arithmetic, backward_step(): return (src_grad.at[cols_blk].add(products), None)  109 us
    scatter-add x11, other arithmetic, forward_step(): summed = summed.at[rows_blk].add(products)  71.1 us
    psum x1, blocking collectives, shards(): lax.psum((self_term, neigh_term, bias_term), ('nodes', 'cols'))  66.2 us
    all_gather x1, waiting for transfers between devices, shards(): source = lax.all_gather(node_feats, 'nodes', axis=0, tiled=True)  48.4 us
    dot_general x11, matrix products, forward_step(): jnp.einsum('tba,tbf->taf', bits_blk, picked, preferred_element_type=jnp.f...  48.1 us
    gather x11, local copies, waits for them, and re-layouts, forward_step(): picked = source_blocks[cols_blk]  39.8 us
    dot_general x11, matrix products, backward_step(): jnp.einsum('tba,taf->tbf', bits_blk, picked, preferred_element_type=jnp.f...  30.1 us
    shift_right_arithmetic x66, local copies, waits for them, and re-layouts, unpack_tiles(): jnp.right_shift(packed[:, :, None, :], shifts[None, None, :, None]) & 1  23.4 us
  transfers between devices with their start and end apart: 5, of which 4 were waited for; matrix products, arithmetic and copies ran while one was open for 31% of the time, Pallas kernels for 0%

commit v1 on v0

--- a/solution.py
+++ b/solution.py
@@ -70,7 +70,7 @@
     neigh_term = jnp.dot(neigh_mean.T, pre_grad, preferred_element_type=jnp.float32)
     bias_term = jnp.sum(pre_grad.astype(jnp.float32), axis=0)
     self_grad, neigh_grad, bias_grad = lax.psum(
-        (self_term, neigh_term, bias_term), ("nodes", "cols")
+        lax.psum((self_term, neigh_term, bias_term), "cols"), "nodes"
     )
     mean_grad = (
         jnp.dot(pre_grad, w_neigh.T, preferred_element_type=jnp.float32) / degree[:, None]

time: 560 us -> 624 us (1.11)
  waiting for transfers between devices: 96.4 us -> 171 us
  blocking collectives: 80 us -> 68.9 us
    psum x1 -> x2, waiting for transfers between devices: 0.01 us -> 58.7 us  [the longest x1 58.7 us: shards(): lax.psum((self_term, neigh_term, bias_term), 'cols')]
    psum x1 -> x2, blocking collectives: 66.2 us -> 55.2 us  [the longest x1 42 us: shards(): lax.psum(lax.psum((self_term, neigh_term, bias_term), 'cols'), 'nodes')]
    reduce_scatter x1, waiting for transfers between devices: 9.32 us -> 20.2 us  [shards(): lax.psum_scatter(src_total, 'nodes', scatter_dimension=0, tiled=True)]
  transfers between devices with their start and end apart: 5 -> 6, of which waited for: 4 -> 5; matrix products, arithmetic and copies ran while one was open for 31% -> 28% of each run, Pallas kernels for 0% -> 0%
where the time goes in v1:
time: 624 us; the launch traced here: 621 us
  other arithmetic  200 us (32%)
  waiting for transfers between devices  171 us (27%)
  matrix products  85.6 us (14%)
  local copies, waits for them, and re-layouts  79.4 us (13%)
  blocking collectives  68.9 us (11%)
  between operations  14.9 us (2%)
    scatter-add x11, other arithmetic, backward_step(): return (src_grad.at[cols_blk].add(products), None)  109 us
    scatter-add x11, other arithmetic, forward_step(): summed = summed.at[rows_blk].add(products)  71.1 us
    psum x1, waiting for transfers between devices, shards(): lax.psum((self_term, neigh_term, bias_term), 'cols')  58.7 us
    all_gather x1, waiting for transfers between devices, shards(): source = lax.all_gather(node_feats, 'nodes', axis=0, tiled=True)  48.4 us
    dot_general x11, matrix products, forward_step(): jnp.einsum('tba,tbf->taf', bits_blk, picked, preferred_element_type=jnp.f...  48.1 us
    psum x1, blocking collectives, shards(): lax.psum(lax.psum((self_term, neigh_term, bias_term), 'cols'), 'nodes')  42 us
    gather x11, local copies, waits for them, and re-layouts, forward_step(): picked = source_blocks[cols_blk]  39.8 us
    dot_general x11, matrix products, backward_step(): jnp.einsum('tba,taf->tbf', bits_blk, picked, preferred_element_type=jnp.f...  30.1 us
  transfers between devices with their start and end apart: 6, of which 5 were waited for; matrix products, arithmetic and copies ran while one was open for 28% of the time, Pallas kernels for 0%

profile of v1, /device:TPU:0, one launch (start us, length us, event | category | flops | bytes accessed | tf_op | source)
XLA Modules:
  0.0 620.7 jit_solution(4193034044587431317)
XLA Ops:
  9.5 48.4 %all-gather.3.cloned.1.call-done = bf16[4096,256]{1,0:T(8,128)(2,1)} async-done(((bf16[256,256]{1,0:T(8,128)(2,1)}), bf16[4096,256]{1,0:T(8,128)(2,1)}) %all-gather.3.cloned.1.call-update) | async-done | bytes 2097168 | tf_op jit(solution)/shard_map/all_gather | solution.py:28
  58.1 182.1 %while.22 = (s32[]{:T(128)}, f32[16,128,256]{2,1,0:T(8,128)S(1)}, f32[16,128]{1,0:T(8,128)S(1)}, s32[11,32]{1,0:T(8,128)S(1)}, s32[11,32,16,128]{3,2,1,0:T(8,128...) while((s32[]{:T(128)}, f32[16,128,256]{2,1,0:T(8,128)S(1)}, ...), condition=%wide.region_4.5_spmd, body=%wide.region_0.4_spmd.sunk | while | flops 272635072 | bytes 24165348 | solution.py:46
  67.2 6.5 %scatter_fusion = f32[16,128,256]{2,1,0:T(8,128)S(1)} fusion(f32[16,128,256]{2,1,0:T(8,128)S(1)} %get-tuple-element.234, s32[32]{0:T(128)S(1)} %get-tuple-element.215, f32[32,128,256]{2,1,0:T(8,128)} %fusion.56), kind=kCustom, calls=%fused_computation.2.clone.1 | custom fusion | flops 1048576 | bytes 12583040 | tf_op jit(solution)/shard_map/while/body/eval_jaxpr/scatter-add | solution.py:38
  83.8 6.5 %scatter_fusion = f32[16,128,256]{2,1,0:T(8,128)S(1)} fusion(f32[16,128,256]{2,1,0:T(8,128)S(1)} %get-tuple-element.234, s32[32]{0:T(128)S(1)} %get-tuple-element.215, f32[32,128,256]{2,1,0:T(8,128)} %fusion.56), kind=kCustom, calls=%fused_computation.2.clone.1 | custom fusion | flops 1048576 | bytes 12583040 | tf_op jit(solution)/shard_map/while/body/eval_jaxpr/scatter-add | solution.py:38
  100.4 6.5 %scatter_fusion = f32[16,128,256]{2,1,0:T(8,128)S(1)} fusion(f32[16,128,256]{2,1,0:T(8,128)S(1)} %get-tuple-element.234, s32[32]{0:T(128)S(1)} %get-tuple-element.215, f32[32,128,256]{2,1,0:T(8,128)} %fusion.56), kind=kCustom, calls=%fused_computation.2.clone.1 | custom fusion | flops 1048576 | bytes 12583040 | tf_op jit(solution)/shard_map/while/body/eval_jaxpr/scatter-add | solution.py:38
  116.9 6.5 %scatter_fusion = f32[16,128,256]{2,1,0:T(8,128)S(1)} fusion(f32[16,128,256]{2,1,0:T(8,128)S(1)} %get-tuple-element.234, s32[32]{0:T(128)S(1)} %get-tuple-element.215, f32[32,128,256]{2,1,0:T(8,128)} %fusion.56), kind=kCustom, calls=%fused_computation.2.clone.1 | custom fusion | flops 1048576 | bytes 12583040 | tf_op jit(solution)/shard_map/while/body/eval_jaxpr/scatter-add | solution.py:38
  133.5 6.5 %scatter_fusion = f32[16,128,256]{2,1,0:T(8,128)S(1)} fusion(f32[16,128,256]{2,1,0:T(8,128)S(1)} %get-tuple-element.234, s32[32]{0:T(128)S(1)} %get-tuple-element.215, f32[32,128,256]{2,1,0:T(8,128)} %fusion.56), kind=kCustom, calls=%fused_computation.2.clone.1 | custom fusion | flops 1048576 | bytes 12583040 | tf_op jit(solution)/shard_map/while/body/eval_jaxpr/scatter-add | solution.py:38
  150.0 6.5 %scatter_fusion = f32[16,128,256]{2,1,0:T(8,128)S(1)} fusion(f32[16,128,256]{2,1,0:T(8,128)S(1)} %get-tuple-element.234, s32[32]{0:T(128)S(1)} %get-tuple-element.215, f32[32,128,256]{2,1,0:T(8,128)} %fusion.56), kind=kCustom, calls=%fused_computation.2.clone.1 | custom fusion | flops 1048576 | bytes 12583040 | tf_op jit(solution)/shard_map/while/body/eval_jaxpr/scatter-add | solution.py:38
  166.6 6.5 %scatter_fusion = f32[16,128,256]{2,1,0:T(8,128)S(1)} fusion(f32[16,128,256]{2,1,0:T(8,128)S(1)} %get-tuple-element.234, s32[32]{0:T(128)S(1)} %get-tuple-element.215, f32[32,128,256]{2,1,0:T(8,128)} %fusion.56), kind=kCustom, calls=%fused_computation.2.clone.1 | custom fusion | flops 1048576 | bytes 12583040 | tf_op jit(solution)/shard_map/while/body/eval_jaxpr/scatter-add | solution.py:38
  183.1 6.5 %scatter_fusion = f32[16,128,256]{2,1,0:T(8,128)S(1)} fusion(f32[16,128,256]{2,1,0:T(8,128)S(1)} %get-tuple-element.234, s32[32]{0:T(128)S(1)} %get-tuple-element.215, f32[32,128,256]{2,1,0:T(8,128)} %fusion.56), kind=kCustom, calls=%fused_computation.2.clone.1 | custom fusion | flops 1048576 | bytes 12583040 | tf_op jit(solution)/shard_map/while/body/eval_jaxpr/scatter-add | solution.py:38
  199.7 6.5 %scatter_fusion = f32[16,128,256]{2,1,0:T(8,128)S(1)} fusion(f32[16,128,256]{2,1,0:T(8,128)S(1)} %get-tuple-element.234, s32[32]{0:T(128)S(1)} %get-tuple-element.215, f32[32,128,256]{2,1,0:T(8,128)} %fusion.56), kind=kCustom, calls=%fused_computation.2.clone.1 | custom fusion | flops 1048576 | bytes 12583040 | tf_op jit(solution)/shard_map/while/body/eval_jaxpr/scatter-add | solution.py:38
  216.2 6.5 %scatter_fusion = f32[16,128,256]{2,1,0:T(8,128)S(1)} fusion(f32[16,128,256]{2,1,0:T(8,128)S(1)} %get-tuple-element.234, s32[32]{0:T(128)S(1)} %get-tuple-element.215, f32[32,128,256]{2,1,0:T(8,128)} %fusion.56), kind=kCustom, calls=%fused_computation.2.clone.1 | custom fusion | flops 1048576 | bytes 12583040 | tf_op jit(solution)/shard_map/while/body/eval_jaxpr/scatter-add | solution.py:38
  232.8 6.5 %scatter_fusion = f32[16,128,256]{2,1,0:T(8,128)S(1)} fusion(f32[16,128,256]{2,1,0:T(8,128)S(1)} %get-tuple-element.234, s32[32]{0:T(128)S(1)} %get-tuple-element.215, f32[32,128,256]{2,1,0:T(8,128)} %fusion.56), kind=kCustom, calls=%fused_computation.2.clone.1 | custom fusion | flops 1048576 | bytes 12583040 | tf_op jit(solution)/shard_map/while/body/eval_jaxpr/scatter-add | solution.py:38
  243.1 13.7 %all-reduce = f32[2048]{0:T(1024)S(1)} all-reduce(f32[2048]{0:T(1024)S(1)} %bitcast.96), channel_id=3, replica_groups=mesh['nodes'=16,'cols'=8] {'cols'}, use_global_device_ids=true, to_apply=%region_6.7.clone | all-reduce | flops 2048 | bytes 16384
  256.9 17.8 %reduce-scatter.3.cloned.1.call-done = f32[256,256]{1,0:T(8,128)} async-done(((f32[2048,256]{1,0:T(8,128)}), f32[256,256]{1,0:T(8,128)}) %reduce-scatter.3.cloned.1.call-update) | async-done | bytes 262160 | tf_op jit(solution)/shard_map/reduce_scatter | solution.py:50
  280.3 58.7 %all-reduce.8.cloned.1.call-done = (f32[256,256]{0,1:T(8,128)}, f32[256,256]{1,0:T(8,128)}) async-done(((f32[256,256]{0,1:T(8,128)}, f32[256,256]{1,0:T(8,128)}), (f32[256,256]{0,1:T(8,128)}, f32[256,256]{1,0:T(8,128)})) %all-reduce.8.cloned.1.call-update) | async-done | bytes 524304 | tf_op jit(solution)/shard_map/psum | solution.py:73
  339.0 24.8 %all-gather.5.cloned.1.call-done = bf16[2048,256]{1,0:T(8,128)(2,1)} async-done(((bf16[256,256]{1,0:T(8,128)(2,1)}), bf16[2048,256]{1,0:T(8,128)(2,1)}) %all-gather.5.cloned.1.call-update) | async-done | bytes 1048592 | tf_op jit(solution)/shard_map/all_gather | solution.py:78
  366.3 166.2 %while.23 = (s32[]{:T(128)}, f32[32,128,256]{2,1,0:T(8,128)}, s32[11,32]{1,0:T(8,128)}, s32[11,32,16,128]{3,2,1,0:T(8,128)}, s32[11,32]{1,0:T(8,128)}, /*index=5*/bf16[16,128,256]{2,1,0:T(8,128)(2,1)S(1)}, s32[]{:T(128)}) while((s32[]{:T(128)}, f32[32,128,256]{2,1,0:T(8,128)}, s32[11,32]{1,0:T(8,128)}, s32[11,32,16,128]{3,2,1,0:T(8,128)}, ...), condition=%wide.region_9.10_spmd, body=%wide.region_7.9_spmd.sunk | while | flops 271058112 | bytes 23862236 | solution.py:88
  371.5 9.8 %scatter_fusion.1 = f32[32,128,256]{2,1,0:T(8,128)} fusion(f32[32,128,256]{2,1,0:T(8,128)} %get-tuple-element.257, s32[32]{0:T(128)S(1)} %get-tuple-element.223, f32[32,128,256]{2,1,0:T(8,128)} %fusion.60), kind=kCustom, calls=%fused_computation.4.clone.1 | custom fusion | flops 1048576 | bytes 12583040 | tf_op jit(solution)/shard_map/while/body/eval_jaxpr/scatter-add | solution.py:86
  386.5 9.9 %scatter_fusion.1 = f32[32,128,256]{2,1,0:T(8,128)} fusion(f32[32,128,256]{2,1,0:T(8,128)} %get-tuple-element.257, s32[32]{0:T(128)S(1)} %get-tuple-element.223, f32[32,128,256]{2,1,0:T(8,128)} %fusion.60), kind=kCustom, calls=%fused_computation.4.clone.1 | custom fusion | flops 1048576 | bytes 12583040 | tf_op jit(solution)/shard_map/while/body/eval_jaxpr/scatter-add | solution.py:86
  401.6 9.9 %scatter_fusion.1 = f32[32,128,256]{2,1,0:T(8,128)} fusion(f32[32,128,256]{2,1,0:T(8,128)} %get-tuple-element.257, s32[32]{0:T(128)S(1)} %get-tuple-element.223, f32[32,128,256]{2,1,0:T(8,128)} %fusion.60), kind=kCustom, calls=%fused_computation.4.clone.1 | custom fusion | flops 1048576 | bytes 12583040 | tf_op jit(solution)/shard_map/while/body/eval_jaxpr/scatter-add | solution.py:86
  416.7 9.9 %scatter_fusion.1 = f32[32,128,256]{2,1,0:T(8,128)} fusion(f32[32,128,256]{2,1,0:T(8,128)} %get-tuple-element.257, s32[32]{0:T(128)S(1)} %get-tuple-element.223, f32[32,128,256]{2,1,0:T(8,128)} %fusion.60), kind=kCustom, calls=%fused_computation.4.clone.1 | custom fusion | flops 1048576 | bytes 12583040 | tf_op jit(solution)/shard_map/while/body/eval_jaxpr/scatter-add | solution.py:86
  431.8 10.0 %scatter_fusion.1 = f32[32,128,256]{2,1,0:T(8,128)} fusion(f32[32,128,256]{2,1,0:T(8,128)} %get-tuple-element.257, s32[32]{0:T(128)S(1)} %get-tuple-element.223, f32[32,128,256]{2,1,0:T(8,128)} %fusion.60), kind=kCustom, calls=%fused_computation.4.clone.1 | custom fusion | flops 1048576 | bytes 12583040 | tf_op jit(solution)/shard_map/while/body/eval_jaxpr/scatter-add | solution.py:86
  446.9 10.0 %scatter_fusion.1 = f32[32,128,256]{2,1,0:T(8,128)} fusion(f32[32,128,256]{2,1,0:T(8,128)} %get-tuple-element.257, s32[32]{0:T(128)S(1)} %get-tuple-element.223, f32[32,128,256]{2,1,0:T(8,128)} %fusion.60), kind=kCustom, calls=%fused_computation.4.clone.1 | custom fusion | flops 1048576 | bytes 12583040 | tf_op jit(solution)/shard_map/while/body/eval_jaxpr/scatter-add | solution.py:86
  462.1 10.1 %scatter_fusion.1 = f32[32,128,256]{2,1,0:T(8,128)} fusion(f32[32,128,256]{2,1,0:T(8,128)} %get-tuple-element.257, s32[32]{0:T(128)S(1)} %get-tuple-element.223, f32[32,128,256]{2,1,0:T(8,128)} %fusion.60), kind=kCustom, calls=%fused_computation.4.clone.1 | custom fusion | flops 1048576 | bytes 12583040 | tf_op jit(solution)/shard_map/while/body/eval_jaxpr/scatter-add | solution.py:86
  477.5 9.9 %scatter_fusion.1 = f32[32,128,256]{2,1,0:T(8,128)} fusion(f32[32,128,256]{2,1,0:T(8,128)} %get-tuple-element.257, s32[32]{0:T(128)S(1)} %get-tuple-element.223, f32[32,128,256]{2,1,0:T(8,128)} %fusion.60), kind=kCustom, calls=%fused_computation.4.clone.1 | custom fusion | flops 1048576 | bytes 12583040 | tf_op jit(solution)/shard_map/while/body/eval_jaxpr/scatter-add | solution.py:86
  492.5 10.0 %scatter_fusion.1 = f32[32,128,256]{2,1,0:T(8,128)} fusion(f32[32,128,256]{2,1,0:T(8,128)} %get-tuple-element.257, s32[32]{0:T(128)S(1)} %get-tuple-element.223, f32[32,128,256]{2,1,0:T(8,128)} %fusion.60), kind=kCustom, calls=%fused_computation.4.clone.1 | custom fusion | flops 1048576 | bytes 12583040 | tf_op jit(solution)/shard_map/while/body/eval_jaxpr/scatter-add | solution.py:86
  507.7 9.9 %scatter_fusion.1 = f32[32,128,256]{2,1,0:T(8,128)} fusion(f32[32,128,256]{2,1,0:T(8,128)} %get-tuple-element.257, s32[32]{0:T(128)S(1)} %get-tuple-element.223, f32[32,128,256]{2,1,0:T(8,128)} %fusion.60), kind=kCustom, calls=%fused_computation.4.clone.1 | custom fusion | flops 1048576 | bytes 12583040 | tf_op jit(solution)/shard_map/while/body/eval_jaxpr/scatter-add | solution.py:86
  522.7 9.8 %scatter_fusion.1 = f32[32,128,256]{2,1,0:T(8,128)} fusion(f32[32,128,256]{2,1,0:T(8,128)} %get-tuple-element.257, s32[32]{0:T(128)S(1)} %get-tuple-element.223, f32[32,128,256]{2,1,0:T(8,128)} %fusion.60), kind=kCustom, calls=%fused_computation.4.clone.1 | custom fusion | flops 1048576 | bytes 12583040 | tf_op jit(solution)/shard_map/while/body/eval_jaxpr/scatter-add | solution.py:86
  533.2 13.2 %psum.46 = f32[256]{0:T(256)S(1)} all-reduce(f32[256]{0:T(256)S(1)} %copy-done.7), channel_id=1, replica_groups=mesh['nodes'=16,'cols'=8] {'cols'}, use_global_device_ids=true, to_apply=%region_16.17 | all-reduce | flops 256 | bytes 2048 | tf_op jit(solution)/shard_map/psum | solution.py:73
  546.4 42.0 %psum.47 = f32[256]{0:T(256)} all-reduce(f32[256]{0:T(256)S(1)} %psum.46), channel_id=1, replica_groups=mesh['nodes'=16,'cols'=8] {'nodes'}, use_global_device_ids=true, to_apply=%region_17.18 | all-reduce | flops 256 | bytes 2048 | tf_op jit(solution)/shard_map/psum | solution.py:72
  590.2 20.2 %reduce-scatter.5.cloned.1.call-done = f32[256,256]{1,0:T(8,128)} async-done(((f32[4096,256]{1,0:T(8,128)}), f32[256,256]{1,0:T(8,128)}) %reduce-scatter.5.cloned.1.call-update) | async-done | bytes 262160 | tf_op jit(solution)/shard_map/reduce_scatter | solution.py:94
  (230 shorter events, 185.9 us)
Async XLA Ops:
  7.2 267.5 %copy-start = (bf16[256,256]{1,0:T(8,128)(2,1)S(1)}, bf16[256,256]{1,0:T(8,128)(2,1)}, u32[]{:S(2)}) copy-start(bf16[256,256]{1,0:T(8,128)(2,1)} %param.17) | copy-start | bytes 393220
  7.2 50.7 %all-gather.3.cloned.1.call-start = ((), (), s32[]{:S(2)}) async-start(), calls=%async_computation.2 | async-start | bytes 2228224 | tf_op jit(solution)/shard_map/all_gather | solution.py:28
  7.9 266.8 %reduce-scatter.3.cloned.1.call-start = ((), (), s32[]{:S(2)}) async-start(), calls=%async_computation.3 | async-start | bytes 2359296 | tf_op jit(solution)/shard_map/reduce_scatter | solution.py:50
  240.2 1.4 copy-start.1
  240.2 2.0 copy-start.5
  240.2 2.0 copy-start.6
  240.3 1.4 copy-start.11
  240.3 2.6 copy-start.3
  240.3 2.6 copy-start.4
  240.3 34.4 %copy-start.9 = (bf16[256,256]{1,0:T(8,128)(2,1)S(1)}, bf16[256,256]{1,0:T(8,128)(2,1)}, u32[]{:S(2)}) copy-start(bf16[256,256]{1,0:T(8,128)(2,1)} %param.19) | copy-start | bytes 393220
  240.3 34.4 %copy-start.10 = (f32[256]{0:T(256)S(1)}, f32[256]{0:T(256)}, u32[]{:S(2)}) copy-start(f32[256]{0:T(256)} %param.18) | copy-start | bytes 3076
  241.6 97.4 %all-reduce.8.cloned.1.call-start = ((), (), s32[]{:S(2)}) async-start(), calls=%async_computation.7 | async-start | bytes 1048576 | tf_op jit(solution)/shard_map/psum | solution.py:73
  274.7 3.5 copy-start.8
  279.3 84.6 %all-gather.5.cloned.1.call-start = ((), (), s32[]{:S(2)}) async-start(), calls=%async_computation.4 | async-start | bytes 1179648 | tf_op jit(solution)/shard_map/all_gather | solution.py:78
  280.2 308.2 %all-reduce.6.cloned.1.call-start = ((), (), s32[]{:S(2)}) async-start(), calls=%async_computation.6 | async-start | bytes 1048576 | tf_op jit(solution)/shard_map/psum | solution.py:72
  339.0 271.3 %reduce-scatter.5.cloned.1.call-start = ((), (), s32[]{:S(2)}) async-start(), calls=%async_computation.5 | async-start | bytes 4456448 | tf_op jit(solution)/shard_map/reduce_scatter | solution.py:94
  363.9 2.4 copy-start.2
  532.5 0.7 copy-start.7
Sparse Core Ops, SparseCore 0:
  10.2 47.7 all-gather.2
  241.7 32.9 reduce-scatter.2
  279.4 59.5 all-reduce.7
  341.2 22.5 all-gather.4
  367.4 85.2 all-reduce.5
  532.7 77.6 reduce-scatter.4
